TPU v7x, 128 devices: a whole 4x4x4 slice. The times are simulated.
128 devices in a mesh: variant: 8 (over z_lo, x), vocab: 16 (over y, z_hi, core).
Axes of the slice: x: 4, y: 4, z: 4 (z_hi: 2, z_lo: 2; z = z_hi * 2 + z_lo), core: 2. Of those that a mesh axis runs over, the one named last changes fastest.
Arguments:
- teacher_hidden: bfloat16 [8, 256, 4096], P(None, None, ('variant', 'vocab')), may hold values from -24 to 24
- teacher_weight: bfloat16 [4096, 64128], P(None, ('vocab', 'variant')), may hold values from -1 to 1
- variant_ids: int32 [8], replicated, may hold values from 0 to 13
- temps: float32 [14], replicated, may hold values from 0.7 to 1.5
- student_hidden: bfloat16 [256, 2048], P(None, 'variant'), may hold values from -24 to 24
- student_weight: bfloat16 [2048, 64128], P('variant', 'vocab'), may hold values from -1 to 1
- token_ids: int32 [256], P('variant'), may hold values from 0 to 64127
- loss_mask: int32 [256], P('variant'), may hold values 0 or 1
Outputs:
- token_loss: float32 [256], P('variant')
- student_grad: float32 [2048, 64128], P('variant', 'vocab')
All inputs are finite; a program needn't handle non-finite values. No bound on the sum of `loss_mask` on one device may be relied on, other than what follows from the above.
Results may differ from a plain program's by a relative error of at most 0.0025.
Values may be sent and summed in bfloat16 or wider, within the bound.
No kernel may reach another device: no remote copies, remote signals or barrier semaphores. Data moves between devices by JAX's collectives and lax.ppermute only.
A program may use at most 192 MiB of HBM per device.

v0:
```python
import jax
import jax.numpy as jnp
from jax import lax
from jax.sharding import PartitionSpec as P

mix_weight = 0.5
loss_scale = 4096.0


def on_device(
    teacher_hidden,
    teacher_weight,
    variant_ids,
    temps,
    student_hidden,
    student_weight,
    token_ids,
    loss_mask,
):
    n_variant = lax.axis_size("variant")
    categories = jnp.arange(temps.shape[0], dtype=jnp.int32)
    taus = jnp.sum(
        jnp.where(variant_ids[:, None] == categories[None, :], temps[None, :], 0.0), axis=1
    )
    hidden_all = lax.all_gather(teacher_hidden, ("variant", "vocab"), axis=2, tiled=True)
    scaled = (
        jnp.einsum("vtd,dc->vtc", hidden_all, teacher_weight, preferred_element_type=jnp.float32)
        / taus[:, None, None]
    )
    local_max = jnp.max(scaled, axis=2)
    top = lax.pmax(local_max, ("variant", "vocab"))
    total = lax.psum(jnp.sum(jnp.exp(scaled - top[:, :, None]), axis=2), ("variant", "vocab"))
    probs = jnp.exp(scaled - top[:, :, None]) / total[:, :, None]
    averaged_cols = jnp.sum(probs, axis=0) / n_variant
    averaged = lax.all_to_all(
        averaged_cols.astype(jnp.bfloat16), "variant", split_axis=0, concat_axis=1, tiled=True
    ).astype(averaged_cols.dtype)
    block = student_hidden
    logits = lax.psum_scatter(
        jnp.dot(block, student_weight, preferred_element_type=jnp.float32),
        "variant",
        scatter_dimension=0,
        tiled=True,
    )
    local_max = jnp.max(logits, axis=1)
    top = lax.pmax(local_max, "vocab")
    total = lax.psum(jnp.sum(jnp.exp(logits - top[:, None]), axis=1), "vocab")
    log_probs = logits - (top + jnp.log(total))[:, None]
    probs_student = jnp.exp(log_probs)
    columns = lax.axis_index("vocab") * logits.shape[1] + jnp.arange(
        logits.shape[1], dtype=jnp.int32
    )
    onehot = token_ids[:, None] == columns[None, :]
    soft, hard = lax.psum(
        (jnp.sum(averaged * log_probs, axis=1), jnp.sum(jnp.where(onehot, log_probs, 0.0), axis=1)),
        "vocab",
    )
    maskf = loss_mask.astype(jnp.float32)
    token_loss = maskf * (-mix_weight * soft - (1.0 - mix_weight) * hard)
    error = (
        loss_scale
        * maskf[:, None]
        * (probs_student - mix_weight * averaged - (1.0 - mix_weight) * onehot.astype(jnp.float32))
    ).astype(jnp.bfloat16)
    block = student_hidden
    student_grad = lax.dot_general(
        block,
        lax.all_gather(error, "variant", axis=0, tiled=True),
        (((0,), (0,)), ((), ())),
        preferred_element_type=jnp.float32,
    )
    return (token_loss, student_grad)


def solution(mesh):
    in_specs = (
        P(None, None, ("variant", "vocab")),
        P(None, ("vocab", "variant")),
        P(),
        P(),
        P(None, "variant"),
        P("variant", "vocab"),
        P("variant"),
        P("variant"),
    )
    out_specs = (P("variant"), P("variant", "vocab"))
    return jax.shard_map(
        on_device, mesh=mesh, in_specs=in_specs, out_specs=out_specs, check_vma=False
    )
```

profile of v0, /device:TPU:0, one launch (start us, length us, event | category | flops | bytes accessed | tf_op | source)
XLA Modules:
  0.0 505.8 jit_solution(16824957268856968234)
XLA Ops:
  8.1 1.5 copy-done
  9.6 3.6 fusion.11
  13.2 0.5 all-gather.3.cloned.1.call-update
  13.8 0.2 select_reduce_fusion
  14.0 60.6 %reduce-scatter.2.cloned.1.call-done = f32[32,4008]{1,0:T(8,128)} async-done(((f32[256,4008]{1,0:T(8,128)}), f32[32,4008]{1,0:T(8,128)}) %reduce-scatter.2.cloned.1.call-update) | async-done | bytes 513040 | tf_op jit(solution)/shard_map/reduce_scatter | solution.py:39
  74.6 1.2 reduce_max.19
  75.8 38.9 %pmax.15 = f32[32]{0:T(128)S(1)} all-reduce(f32[32]{0:T(128)S(1)} %reduce_max.19), channel_id=1, replica_groups=mesh['variant'=8,'vocab'=16] {'vocab'}, use_global_device_ids=true, to_apply=%region_8.9 | all-reduce | flops 32 | bytes 256 | tf_op jit(solution)/shard_map/pmax | solution.py:46
  114.7 151.1 %all-gather.3.cloned.1.call-done = bf16[8,256,4096]{1,2,0:T(8,128)(2,1)} async-done(((bf16[8,256,32]{1,2,0:T(8,128)(2,1)}), bf16[8,256,4096]{1,2,0:T(8,128)(2,1)}) %all-gather.3.cloned.1.call-update) | async-done | bytes 16777232 | tf_op jit(solution)/shard_map/all_gather | solution.py:25
  265.9 14.8 %fusion.10 = (f32[8,256]{1,0:T(8,128)S(1)}, f32[8,256,501]{1,2,0:T(8,128)}) fusion(f32[8]{0:T(128)S(1)} %select_reduce_fusion, bf16[8,256,4096]{1,2,0:T(8,128)(2,1)} %all-gather.3.cloned.1.call-done, bf16[4096,501]{0,1:T(8,128)(2,1)} %param.9), kind=kOutput, calls=%fused_computation.23 | convolution fusion | flops 8407435264 | bytes 24993824 | tf_op jit(solution)/shard_map/vtd,dc->vtc/dot_general | solution.py:27
  280.6 62.0 %pmax.14 = f32[8,256]{1,0:T(8,128)S(1)} all-reduce(f32[8,256]{1,0:T(8,128)S(1)} %get-tuple-element.7), channel_id=1, replica_groups=mesh['variant'=8,'vocab'=16] {'variant','vocab'}, use_global_device_ids=true, to_apply=%region_2.3 | all-reduce | flops 2048 | bytes 16384 | tf_op jit(solution)/shard_map/pmax | solution.py:31
  342.6 2.7 fusion.2
  345.4 64.6 %psum.28 = f32[8,256]{1,0:T(8,128)S(1)} all-reduce(f32[8,256]{1,0:T(8,128)S(1)} %fusion.2), channel_id=1, replica_groups=mesh['variant'=8,'vocab'=16] {'variant','vocab'}, use_global_device_ids=true, to_apply=%region_4.5 | all-reduce | flops 2048 | bytes 16384 | tf_op jit(solution)/shard_map/psum | solution.py:32
  410.0 2.9 divide_reduce_fusion
  413.0 0.8 copy.13
  413.8 3.4 all-to-all-start
  417.3 0.3 exponential_reduce_fusion
  417.6 34.1 %psum.29 = f32[32]{0:T(128)S(1)} all-reduce(f32[32]{0:T(128)S(1)} %exponential_reduce_fusion), channel_id=1, replica_groups=mesh['variant'=8,'vocab'=16] {'vocab'}, use_global_device_ids=true, to_apply=%region_10.11 | all-reduce | flops 32 | bytes 256 | tf_op jit(solution)/shard_map/psum | solution.py:47
  451.8 1.1 copy.14
  452.9 1.4 reshape.27
  454.2 1.1 multiply_reduce_fusion
  455.4 33.7 %all-reduce = (f32[32]{0:T(128)S(1)}, f32[32]{0:T(128)S(1)}) all-reduce(f32[32]{0:T(128)S(1)} %get-tuple-element.3, f32[32]{0:T(128)S(1)} %get-tuple-element.2), channel_id=1, replica_groups=mesh['variant'=8,'vocab'=16] {'vocab'}, use_global_device_ids=true, to_apply=%region_14.15 | all-reduce | flops 64 | bytes 512 | tf_op jit(solution)/shard_map/psum | solution.py:54
  489.1 0.5 subtract_multiply_fusion
  489.6 4.4 all-gather.5.cloned.1.call-done
  494.0 4.3 convolution_bitcast_fusion
  (24 shorter events, 0.3 us)
Async XLA Ops:
  8.0 1.6 copy-start
  8.0 5.8 %copy-start.5 = (f32[14]{0:T(128)S(1)}, f32[14]{0:T(128)}, u32[]{:S(2)}) copy-start(f32[14]{0:T(128)} %param.11) | copy-start | bytes 172
  8.0 5.8 %copy-start.6 = (s32[8]{0:T(128)S(1)}, s32[8]{0:T(128)}, u32[]{:S(2)}) copy-start(s32[8]{0:T(128)} %param.10) | copy-start | bytes 100
  8.0 5.9 %copy-start.4 = (s32[32]{0:T(128)S(1)}, s32[32]{0:T(128)}, u32[]{:S(2)}) copy-start(s32[32]{0:T(128)} %param.15) | copy-start | bytes 388
  8.0 66.6 %reduce-scatter.2.cloned.1.call-start = ((), (), s32[]{:S(2)}) async-start(), calls=%async_computation.3 | async-start | bytes 4718592 | tf_op jit(solution)/shard_map/reduce_scatter | solution.py:39
  13.2 252.7 %all-gather.3.cloned.1.call-start = ((), (), s32[]{:S(2)}) async-start(), calls=%async_computation.2 | async-start | bytes 16908288 | tf_op jit(solution)/shard_map/all_gather | solution.py:25
  345.4 71.9 %copy-start.1 = (f32[32,4008]{1,0:T(8,128)S(1)}, f32[32,4008]{1,0:T(8,128)}, u32[]{:S(2)}) copy-start(f32[32,4008]{1,0:T(8,128)} %reduce-scatter.2.cloned.1.call-done) | copy-start | bytes 1539076
  410.0 44.2 %copy-start.3 = (s32[32]{0:T(128)S(1)}, s32[32]{0:T(128)}, u32[]{:S(2)}) copy-start(s32[32]{0:T(128)} %param.14) | copy-start | bytes 388
  412.9 81.1 %copy-start.2 = (bf16[256,256]{1,0:T(8,128)(2,1)S(1)}, bf16[256,256]{1,0:T(8,128)(2,1)}, u32[]{:S(2)}) copy-start(bf16[256,256]{1,0:T(8,128)(2,1)} %param.12) | copy-start | bytes 393220
  413.8 37.9 %all-to-all-start = ((bf16[8,32,501]{2,1,0:T(8,128)(2,1)}), bf16[8,32,501]{2,1,0:T(8,128)(2,1)S(1)}, u32[]{:S(2)}, u32[]{:S(2)}) async-start(bf16[8,32,501]{2,1,0:T(8,128)(2,1)} %bitcast.1), calls=%async_computation | async-start | bytes 524288 | tf_op jit(solution)/shard_map/all_to_all | solution.py:35
  417.3 76.8 %all-gather.5.cloned.1.call-start = ((), (), s32[]{:S(2)}) async-start(), calls=%async_computation.4 | async-start | bytes 2359296 | tf_op jit(solution)/shard_map/all_gather | solution.py:68
Sparse Core Ops, SparseCore 0:
  13.3 61.2 reduce-scatter.1
  455.5 38.4 all-gather.4
Sparse Core Ops, SparseCore 1:
  15.4 250.4 all-gather.2
where the time goes:
time: 506 us
  blocking collectives  233 us (46%)
  waiting for transfers between devices  217 us (43%)
  matrix products  22.7 us (4%)
  between operations  15.6 us (3%)
  other arithmetic  9.06 us (2%)
    all_gather x1, waiting for transfers between devices, on_device(): lax.all_gather(teacher_hidden, ('variant', 'vocab'), axis=2, tiled=True)  151 us
    psum x1, blocking collectives, on_device(): lax.psum(jnp.sum(jnp.exp(scaled - top[:, :, None]), axis=2), ('variant',...  64.6 us
    pmax x1, blocking collectives, on_device(): top = lax.pmax(local_max, ('variant', 'vocab'))  62 us
    reduce_scatter x1, waiting for transfers between devices, on_device(): lax.psum_scatter(jnp.dot(block, student_weight, preferred_element_type=jn...  60.6 us
    pmax x1, blocking collectives, on_device(): top = lax.pmax(local_max, 'vocab')  38.9 us
    psum x1, blocking collectives, on_device(): total = lax.psum(jnp.sum(jnp.exp(logits - top[:, None]), axis=1), 'vocab')  34.1 us
    psum x1, blocking collectives, on_device(): lax.psum((jnp.sum(averaged * log_probs, axis=1), jnp.sum(jnp.where(onehot...  33.7 us
    dot_general x1, matrix products, on_device(): jnp.einsum('vtd,dc->vtc', hidden_all, teacher_weight, preferred_element_t...  14.8 us
  transfers between devices with their start and end apart: 4, of which 3 were waited for; matrix products, arithmetic and copies ran while one was open for 0% of the time, Pallas kernels for 0%

commit v1 on v0

--- a/solution.py
+++ b/solution.py
@@ -44,7 +44,9 @@
     )
     local_max = jnp.max(logits, axis=1)
     top = lax.pmax(local_max, "vocab")
-    total = lax.psum(jnp.sum(jnp.exp(logits - top[:, None]), axis=1), "vocab")
+    mine = jnp.sum(jnp.exp(logits - top[:, None]), axis=1)
+    state_now = lax.all_gather(mine, "vocab")
+    total = jnp.sum(state_now, axis=0)
     log_probs = logits - (top + jnp.log(total))[:, None]
     probs_student = jnp.exp(log_probs)
     columns = lax.axis_index("vocab") * logits.shape[1] + jnp.arange(

time: 506 us -> 506 us (level)
    unnamed x0 -> x1, blocking collectives: none -> 34.1 us
    psum x1 -> x0, blocking collectives: 34.1 us -> none  [on_device(): total = lax.psum(jnp.sum(jnp.exp(logits - top[:, None]), axis=1), 'vocab')]
  transfers between devices with their start and end apart: 4 -> 4, of which waited for: 3 -> 3; matrix products, arithmetic and copies ran while one was open for 0% -> 1% of each run, Pallas kernels for 0% -> 0%
where the time goes in v1:
time: 506 us
  blocking collectives  234 us (46%)
  waiting for transfers between devices  214 us (42%)
  matrix products  22.7 us (4%)
  between operations  16.3 us (3%)
  other arithmetic  10.2 us (2%)
  local copies, waits for them, and re-layouts  5.73 us (1%)
    all_gather x1, waiting for transfers between devices, on_device(): lax.all_gather(teacher_hidden, ('variant', 'vocab'), axis=2, tiled=True)  149 us
    psum x1, blocking collectives, on_device(): lax.psum(jnp.sum(jnp.exp(scaled - top[:, :, None]), axis=2), ('variant',...  64.6 us
    pmax x1, blocking collectives, on_device(): top = lax.pmax(local_max, ('variant', 'vocab'))  62.3 us
    reduce_scatter x1, waiting for transfers between devices, on_device(): lax.psum_scatter(jnp.dot(block, student_weight, preferred_element_type=jn...  59.4 us
    pmax x1, blocking collectives, on_device(): top = lax.pmax(local_max, 'vocab')  38.9 us
    unnamed x1, blocking collectives  34.1 us
    psum x1, blocking collectives, on_device(): lax.psum((jnp.sum(averaged * log_probs, axis=1), jnp.sum(jnp.where(onehot...  33.7 us
    dot_general x1, matrix products, on_device(): jnp.einsum('vtd,dc->vtc', hidden_all, teacher_weight, preferred_element_t...  14.8 us
  transfers between devices with their start and end apart: 4, of which 3 were waited for; matrix products, arithmetic and copies ran while one was open for 1% of the time, Pallas kernels for 0%

profile of v1, /device:TPU:0, one launch (start us, length us, event | category | flops | bytes accessed | tf_op | source)
XLA Modules:
  0.0 505.6 jit_solution(6001449348035575898)
XLA Ops:
  8.1 1.5 copy-done
  9.6 3.6 fusion.11
  13.2 0.5 all-gather.4.cloned.1.call-update
  13.8 0.6 dynamic-slice
  15.2 59.4 %reduce-scatter.2.cloned.1.call-done = f32[32,4008]{1,0:T(8,128)} async-done(((f32[256,4008]{1,0:T(8,128)}), f32[32,4008]{1,0:T(8,128)}) %reduce-scatter.2.cloned.1.call-update) | async-done | bytes 513040 | tf_op jit(solution)/shard_map/reduce_scatter | solution.py:39
  74.6 1.2 reduce_max.19
  75.8 38.9 %pmax.15 = f32[32]{0:T(128)S(1)} all-reduce(f32[32]{0:T(128)S(1)} %reduce_max.19), channel_id=1, replica_groups=mesh['variant'=8,'vocab'=16] {'vocab'}, use_global_device_ids=true, to_apply=%region_8.9 | all-reduce | flops 32 | bytes 256 | tf_op jit(solution)/shard_map/pmax | solution.py:46
  114.7 1.3 exponential_reduce_fusion
  116.3 149.2 %all-gather.4.cloned.1.call-done = bf16[8,256,4096]{1,2,0:T(8,128)(2,1)} async-done(((bf16[8,256,32]{1,2,0:T(8,128)(2,1)}), bf16[8,256,4096]{1,2,0:T(8,128)(2,1)}) %all-gather.4.cloned.1.call-update) | async-done | bytes 16777232 | tf_op jit(solution)/shard_map/all_gather | solution.py:25
  265.5 14.8 %fusion.10 = (f32[8,256]{1,0:T(8,128)S(1)}, f32[8,256,501]{1,2,0:T(8,128)}) fusion(f32[8]{0:T(128)S(1)} %select_reduce_fusion, bf16[8,256,4096]{1,2,0:T(8,128)(2,1)} %all-gather.4.cloned.1.call-done, bf16[4096,501]{0,1:T(8,128)(2,1)} %param.9), kind=kOutput, calls=%fused_computation.23 | convolution fusion | flops 8407435264 | bytes 24993824 | tf_op jit(solution)/shard_map/vtd,dc->vtc/dot_general | solution.py:27
  280.2 62.3 %pmax.14 = f32[8,256]{1,0:T(8,128)S(1)} all-reduce(f32[8,256]{1,0:T(8,128)S(1)} %get-tuple-element.7), channel_id=1, replica_groups=mesh['variant'=8,'vocab'=16] {'variant','vocab'}, use_global_device_ids=true, to_apply=%region_2.3 | all-reduce | flops 2048 | bytes 16384 | tf_op jit(solution)/shard_map/pmax | solution.py:31
  342.5 2.7 fusion.2
  345.3 64.6 %psum.21 = f32[8,256]{1,0:T(8,128)S(1)} all-reduce(f32[8,256]{1,0:T(8,128)S(1)} %fusion.2), channel_id=1, replica_groups=mesh['variant'=8,'vocab'=16] {'variant','vocab'}, use_global_device_ids=true, to_apply=%region_4.5 | all-reduce | flops 2048 | bytes 16384 | tf_op jit(solution)/shard_map/psum | solution.py:32
  409.9 3.0 divide_reduce_fusion
  413.0 0.8 copy.13
  413.8 3.4 all-to-all-start
  417.3 34.1 %all-reduce = f32[512]{0:T(512)S(1)} all-reduce(f32[512]{0:T(512)S(1)} %dynamic-update-slice), channel_id=2, replica_groups=mesh['variant'=8,'vocab'=16] {'vocab'}, use_global_device_ids=true, to_apply=%add | all-reduce | flops 512 | bytes 4096
  451.6 1.1 copy.14
  452.7 1.4 reshape.27
  454.1 1.1 multiply_reduce_fusion
  455.2 33.7 %all-reduce.1 = (f32[32]{0:T(128)S(1)}, f32[32]{0:T(128)S(1)}) all-reduce(f32[32]{0:T(128)S(1)} %get-tuple-element.3, f32[32]{0:T(128)S(1)} %get-tuple-element.2), channel_id=1, replica_groups=mesh['variant'=8,'vocab'=16] {'vocab'}, use_global_device_ids=true, to_apply=%region_14.15 | all-reduce | flops 64 | bytes 512 | tf_op jit(solution)/shard_map/psum | solution.py:56
  488.9 0.5 subtract_multiply_fusion
  489.4 4.4 all-gather.6.cloned.1.call-done
  493.8 4.3 convolution_bitcast_fusion
  (31 shorter events, 0.8 us)
Async XLA Ops:
  8.0 1.6 copy-start
  8.0 5.8 %copy-start.7 = (u32[128]{0:T(128)S(1)}, u32[128]{0:T(128)}, u32[]{:S(2)}) copy-start(u32[128]{0:T(128)} %constant.26) | copy-start | bytes 1540
  8.0 7.0 %copy-start.5 = (f32[14]{0:T(128)S(1)}, f32[14]{0:T(128)}, u32[]{:S(2)}) copy-start(f32[14]{0:T(128)} %param.11) | copy-start | bytes 172
  8.0 7.0 %copy-start.6 = (s32[8]{0:T(128)S(1)}, s32[8]{0:T(128)}, u32[]{:S(2)}) copy-start(s32[8]{0:T(128)} %param.10) | copy-start | bytes 100
  8.0 7.2 %copy-start.4 = (s32[32]{0:T(128)S(1)}, s32[32]{0:T(128)}, u32[]{:S(2)}) copy-start(s32[32]{0:T(128)} %param.15) | copy-start | bytes 388
  8.1 66.5 %reduce-scatter.2.cloned.1.call-start = ((), (), s32[]{:S(2)}) async-start(), calls=%async_computation.3 | async-start | bytes 4718592 | tf_op jit(solution)/shard_map/reduce_scatter | solution.py:39
  13.2 252.3 %all-gather.4.cloned.1.call-start = ((), (), s32[]{:S(2)}) async-start(), calls=%async_computation.2 | async-start | bytes 16908288 | tf_op jit(solution)/shard_map/all_gather | solution.py:25
  409.9 44.2 %copy-start.1 = (f32[32,4008]{1,0:T(8,128)S(1)}, f32[32,4008]{1,0:T(8,128)}, u32[]{:S(2)}) copy-start(f32[32,4008]{1,0:T(8,128)} %reduce-scatter.2.cloned.1.call-done) | copy-start | bytes 1539076
  409.9 44.2 %copy-start.3 = (s32[32]{0:T(128)S(1)}, s32[32]{0:T(128)}, u32[]{:S(2)}) copy-start(s32[32]{0:T(128)} %param.14) | copy-start | bytes 388
  412.9 80.9 %copy-start.2 = (bf16[256,256]{1,0:T(8,128)(2,1)S(1)}, bf16[256,256]{1,0:T(8,128)(2,1)}, u32[]{:S(2)}) copy-start(bf16[256,256]{1,0:T(8,128)(2,1)} %param.12) | copy-start | bytes 393220
  413.8 37.7 %all-to-all-start = ((bf16[8,32,501]{2,1,0:T(8,128)(2,1)}), bf16[8,32,501]{2,1,0:T(8,128)(2,1)S(1)}, u32[]{:S(2)}, u32[]{:S(2)}) async-start(bf16[8,32,501]{2,1,0:T(8,128)(2,1)} %bitcast.1), calls=%async_computation | async-start | bytes 524288 | tf_op jit(solution)/shard_map/all_to_all | solution.py:35
  417.2 76.6 %all-gather.6.cloned.1.call-start = ((), (), s32[]{:S(2)}) async-start(), calls=%async_computation.4 | async-start | bytes 2359296 | tf_op jit(solution)/shard_map/all_gather | solution.py:70
Sparse Core Ops, SparseCore 0:
  13.3 61.2 reduce-scatter.1
  455.4 38.4 all-gather.5
Sparse Core Ops, SparseCore 1:
  15.4 250.0 all-gather.3
